TPU v7x, 32 devices: a whole 2x2x4 slice. The times are simulated.
32 devices in a mesh: parts: 2 (over y), rows: 4 (over x, core), cols: 4 (over z).
Axes of the slice: x: 2, y: 2, z: 4, core: 2. Of those that a mesh axis runs over, the one named last changes fastest.
Arguments:
- pair: float32 [256, 4, 32, 128], P(('parts', 'rows'), None, 'cols'), parts along dimension 0, may hold values from -6 to 6
- singles: float32 [256, 384], P(('parts', 'rows')), parts along dimension 0, may hold values from -6 to 6
- restype: int32 [256], P(('parts', 'rows')), parts along dimension 0, may hold values from 0 to 31
- block_mask: int32 [32, 4, 4], P(('parts', 'rows'), None, 'cols'), parts along dimension 0, may hold values from 0 to 1, as said below
- ln_trans: float32 [128], replicated, may hold values from 0.1 to 1.9
- w_trans_in: bfloat16 [128, 1024], replicated, may hold values from -0.5 to 0.5
- w_trans_out: bfloat16 [512, 128], replicated, may hold values from -0.25 to 0.25
- ln_bias: float32 [128], replicated, may hold values from 0.1 to 1.9
- w_bias: bfloat16 [128, 16], replicated, may hold values from -0.5 to 0.5
- restype_table: float32 [32, 384], replicated, may hold values from -6 to 6
- ln_single: float32 [384], replicated, may hold values from 0.1 to 1.9
- w_attn: bfloat16 [384, 1536], replicated, may hold values from -80 to 80
- w_single_out: bfloat16 [384, 384], replicated, may hold values from -0.3125 to 0.3125
- w_dist: bfloat16 [128, 64], replicated, may hold values from -0.5 to 0.5
- dist_bias: float32 [64], replicated, may hold values from -6 to 6
Outputs:
- pair_next: float32 [256, 4, 32, 128], P(('parts', 'rows'), None, 'cols'), parts along dimension 0
- singles_next: float32 [256, 384], P(('parts', 'rows')), parts along dimension 0
- dist_logits: float32 [256, 4, 2048], P(('parts', 'rows'), None, 'cols'), parts along dimension 0
There are 2 independent parts, one for each index of `parts`. A program takes and returns all parts, laid end to end along the dimension named above; an argument that names none is the same for every part. Nothing has to cross between parts.
Inputs may be any that keep to these rules, and one draw needn't show every extreme that they name: block_mask[p, a, c] is 1 where p == a * 4 + c.
All inputs are finite; a program needn't handle non-finite values.
Results may differ from a plain program's by a relative error of at most 0.0044.
Values may be sent and summed in bfloat16 or wider, within the bound.
No kernel may reach another device: no remote copies, remote signals or barrier semaphores. Data moves between devices by JAX's collectives and lax.ppermute only.
A program may use at most 64 MiB of HBM per device.

v0:
```python
import math
import jax
import jax.numpy as jnp
from jax import lax
from jax.sharding import PartitionSpec as P

eps_norm = 1e-05


def layer_norm(values, gain_vec):
    average = jnp.mean(values, axis=-1, keepdims=True)
    centred = values - average
    spread = jnp.mean(centred * centred, axis=-1, keepdims=True)
    return centred * lax.rsqrt(spread + eps_norm) * gain_vec


def pair_block(pair_rows, ln_trans, w_trans_in, w_trans_out, ln_bias, w_bias, w_dist):
    hidden_units = w_trans_out.shape[0]
    normed = layer_norm(pair_rows, ln_trans).astype(jnp.bfloat16)
    gate_up = jnp.dot(normed, w_trans_in, preferred_element_type=jnp.float32)
    hidden = (jax.nn.silu(gate_up[:, :hidden_units]) * gate_up[:, hidden_units:]).astype(
        jnp.bfloat16
    )
    updated = pair_rows + jnp.dot(hidden, w_trans_out, preferred_element_type=jnp.float32)
    biased = layer_norm(updated, ln_bias).astype(jnp.bfloat16)
    head_bias = jnp.dot(biased, w_bias, preferred_element_type=jnp.float32)
    binned = jnp.dot(
        updated.astype(jnp.bfloat16), w_dist, preferred_element_type=jnp.float32
    ).astype(jnp.bfloat16)
    return (updated, head_bias, binned)


def local(
    pair,
    singles,
    restype,
    block_mask,
    ln_trans,
    w_trans_in,
    w_trans_out,
    ln_bias,
    w_bias,
    restype_table,
    ln_single,
    w_attn,
    w_single_out,
    w_dist,
    dist_bias,
):
    queries, key_groups, block_len, channels = pair.shape
    key_count = key_groups * block_len
    q_groups = queries // block_len
    head_count = w_bias.shape[1]
    model_width = w_single_out.shape[0]
    head_width = model_width // head_count
    bin_count = w_dist.shape[1]
    step_rows = math.gcd(queries, 16)
    pair_tiles = pair.reshape(queries // step_rows, step_rows * key_count, channels)

    def run_tile(pair_tile):
        return pair_block(pair_tile, ln_trans, w_trans_in, w_trans_out, ln_bias, w_bias, w_dist)

    updated, head_bias, binned = lax.map(run_tile, pair_tiles)
    pair_next = updated.reshape(queries, key_groups, block_len, channels)
    head_bias = head_bias.reshape(queries, key_count, head_count)
    binned = binned.reshape(queries, key_groups, block_len, bin_count)
    type_count = restype_table.shape[0]
    one_hot = (restype[:, None] == jnp.arange(type_count, dtype=jnp.int32)[None, :]).astype(
        jnp.float32
    )
    embedded = singles + jnp.dot(one_hot, restype_table, precision=lax.Precision.HIGHEST)
    normed_s = layer_norm(embedded, ln_single).astype(jnp.bfloat16)
    query_proj = (
        jnp.dot(normed_s, w_attn[:, :model_width], preferred_element_type=jnp.float32)
        * head_width ** (-0.5)
    ).astype(jnp.bfloat16)
    gate_vals = jax.nn.sigmoid(
        jnp.dot(normed_s, w_attn[:, 3 * model_width :], preferred_element_type=jnp.float32)
    )
    key_weights = w_attn[:, model_width : 3 * model_width]
    own_rows = lax.dynamic_slice_in_dim(normed_s, lax.axis_index("cols") * block_len, block_len, 0)
    local_kv = jnp.dot(own_rows, key_weights, preferred_element_type=jnp.float32).astype(
        jnp.bfloat16
    )
    key_values = lax.all_gather(local_kv, "rows", axis=0, tiled=True)
    q_heads = query_proj.reshape(queries, head_count, head_width)
    k_heads = key_values[:, :model_width].reshape(key_count, head_count, head_width)
    v_heads = key_values[:, model_width:].reshape(key_count, head_count, head_width)
    scores = jnp.einsum("qhd,khd->hqk", q_heads, k_heads, preferred_element_type=jnp.float32)
    scores = scores + jnp.transpose(head_bias, (2, 0, 1))
    allowed = (
        jnp.broadcast_to(
            block_mask[:, None, :, :], (q_groups, block_len, key_groups, block_len)
        ).reshape(queries, key_count)
        > 0
    )
    scores = jnp.where(allowed[None], scores, jnp.float32(-1000000000.0))
    local_max = jnp.max(scores, axis=-1)
    row_max = lax.pmax(local_max, "cols")
    expo = jnp.exp(scores - row_max[:, :, None])
    totals = jnp.sum(expo, axis=-1)
    weighted = jnp.einsum(
        "hqk,khd->qhd", expo.astype(jnp.bfloat16), v_heads, preferred_element_type=jnp.float32
    ).reshape(queries, model_width)
    totals, weighted = (
        lax.psum(totals.astype(jnp.bfloat16), "cols").astype(jnp.float32),
        lax.psum(weighted.astype(jnp.bfloat16), "cols").astype(jnp.float32),
    )
    normalised = (
        weighted.reshape(queries, head_count, head_width) / jnp.transpose(totals)[:, :, None]
    )
    attended = (gate_vals * normalised.reshape(queries, model_width)).astype(jnp.bfloat16)
    singles_next = embedded + jnp.dot(attended, w_single_out, preferred_element_type=jnp.float32)
    grouped = binned.reshape(q_groups, block_len, key_groups, block_len * bin_count)
    outgoing = jnp.transpose(grouped, (2, 0, 1, 3)).reshape(
        key_groups * q_groups, 1, block_len, block_len * bin_count
    )
    arrived = lax.all_to_all(outgoing, ("rows", "cols"), split_axis=0, concat_axis=1, tiled=True)
    mirrored = jnp.transpose(
        arrived.reshape(key_groups, q_groups, block_len, block_len, bin_count), (1, 3, 0, 2, 4)
    )
    mirrored = mirrored.reshape(queries, key_groups, block_len, bin_count)
    logits = binned.astype(jnp.float32) + mirrored.astype(jnp.float32) + dist_bias
    dist_logits = logits.reshape(queries, key_groups, block_len * bin_count)
    return (pair_next, singles_next, dist_logits)


def solution(mesh):
    return jax.shard_map(
        local,
        mesh=mesh,
        in_specs=(
            P(("parts", "rows"), None, "cols", None),
            P(("parts", "rows"), None),
            P(("parts", "rows")),
            P(("parts", "rows"), None, "cols"),
            P(),
            P(),
            P(),
            P(),
            P(),
            P(),
            P(),
            P(),
            P(),
            P(),
            P(),
        ),
        out_specs=(
            P(("parts", "rows"), None, "cols", None),
            P(("parts", "rows"), None),
            P(("parts", "rows"), None, "cols"),
        ),
        check_vma=False,
    )
```

profile of v0, /device:TPU:0, one launch (start us, length us, event | category | flops | bytes accessed | tf_op | source)
XLA Modules:
  0.0 56.2 jit_solution(419873935561623359)
XLA Ops:
  0.6 0.0 copy-start
  0.7 8.1 %while.14 = (s32[]{:T(128)}, f32[2,512,128]{2,1,0:T(8,128)S(1)}, f32[2,512,16]{1,0,2:T(2,128)S(1)}, bf16[2,512,64]{1,2,0:T(8,128)(2,1)S(1)}, f32[2,512,128]{2,1,...) while((s32[]{:T(128)}, f32[2,512,128]{2,1,0:T(8,128)S(1)}, ...), condition=%wide.region_5.6_spmd, body=%wide.region_0.5_spmd.sunk | while | flops 214598656 | bytes 10466621 | solution.py:63
  0.7 1.1 %fusion.65 = (f32[512]{0:T(512)S(1)}, f32[1,512,128]{2,1,0:T(8,128)S(1)}) fusion(f32[2,512,128]{2,1,0:T(8,128)} %get-tuple-element.248, s32[]{:T(128)S(6)} %copy.112), kind=kLoop, calls=%fused_computation.63.clone.1 | loop fusion | flops 65024 | bytes 526340 | tf_op jit(solution)/shard_map/while/body/eval_jaxpr/reduce_sum | solution.py:11
  1.9 0.1 copy.102
  2.0 0.1 multiply_reduce_fusion.5
  2.1 0.0 copy-start.14
  2.1 0.5 fusion.66
  2.6 0.4 copy-done.14
  3.0 0.5 fusion.67
  3.5 0.0 copy-start.3
  3.5 0.1 copy.103
  3.7 0.1 multiply_reduce_fusion.6
  3.7 0.4 copy-done.4
  4.1 0.2 convolution_bitcast_fusion.2
  4.4 0.2 dynamic_update_slice.19
  4.6 0.2 fusion.68
  4.8 1.1 %fusion.65 = (f32[512]{0:T(512)S(1)}, f32[1,512,128]{2,1,0:T(8,128)S(1)}) fusion(f32[2,512,128]{2,1,0:T(8,128)} %get-tuple-element.248, s32[]{:T(128)S(6)} %copy.112), kind=kLoop, calls=%fused_computation.63.clone.1 | loop fusion | flops 65024 | bytes 526340 | tf_op jit(solution)/shard_map/while/body/eval_jaxpr/reduce_sum | solution.py:11
  5.9 0.1 copy.102
  6.1 0.1 multiply_reduce_fusion.5
  6.2 0.5 fusion.66
  6.7 0.4 copy-done.14
  7.0 0.5 fusion.67
  7.5 0.1 copy.103
  7.7 0.1 multiply_reduce_fusion.6
  7.8 0.4 copy-done.4
  8.2 0.2 convolution_bitcast_fusion.2
  8.4 0.2 dynamic_update_slice.19
  8.6 0.2 fusion.68
  8.8 0.0 copy-start.13
  8.9 0.2 copy.80
  9.0 0.2 reshape_reshape.3
  9.2 0.7 %copy.81 = bf16[4,4,8,512]{3,2,1,0:T(8,128)(2,1)} copy(bf16[4,4,8,512]{3,0,2,1:T(4,128)(2,1)S(1)} %bitcast.74) | data formatting | bytes 262144 | tf_op jit(solution)/shard_map/transpose | solution.py:115
  9.9 7.4 %all-to-all-start = ((bf16[16,1,8,512]{3,2,1,0:T(8,128)(2,1)}), bf16[16,1,8,512]{3,2,1,0:T(8,128)(2,1)S(1)}, u32[]{:S(2)}, u32[]{:S(2)}) async-start(bf16[16,1,8,512]{3,2,1,0:T(8,128)(2,1)} %bitcast.16), calls=%async_computation | async-start | bytes 262144 | tf_op jit(solution)/shard_map/all_to_all | solution.py:118
  17.3 0.3 fusion.38
  17.7 0.2 multiply_reduce_fusion.2
  17.8 0.2 reshape.108
  18.0 0.1 copy.74
  18.2 0.1 multiply_convert_fusion.4
  18.3 0.2 fusion.18
  18.4 0.1 copy.87
  18.6 0.2 convolution_convert_fusion.2
  18.7 5.3 %all_gather.3 = bf16[32,768]{1,0:T(8,128)(2,1)S(1)} all-gather(bf16[8,768]{1,0:T(8,128)(2,1)S(1)} %convolution_convert_fusion.2), channel_id=1, replica_groups=mesh['parts'=2,'rows'=4,'cols'=4] {'rows'}, dimensions={0}, use_global_device_ids=true | all-gather | bytes 61440 | tf_op jit(solution)/shard_map/all_gather | solution.py:85
  24.1 0.1 copy.88
  24.2 0.1 copy.86
  24.3 0.1 broadcast_in_dim.41
  24.4 0.1 gt.20
  24.5 0.3 fusion.39
  24.8 12.1 %pmax.7 = f32[16,32]{1,0:T(8,128)S(1)} all-reduce(f32[16,32]{1,0:T(8,128)S(1)} %get-tuple-element.141), channel_id=1, replica_groups=mesh['parts'=2,'rows'=4,'cols'=4] {'cols'}, use_global_device_ids=true, to_apply=%region_9.10 | all-reduce | flops 512 | bytes 4096 | tf_op jit(solution)/shard_map/pmax | solution.py:99
  36.9 0.1 copy.85
  37.0 0.2 convolution_convert_fusion.1
  37.3 0.1 fusion.24
  37.3 0.1 copy.79
  37.5 0.1 copy.89
  37.6 15.8 %all-reduce = (bf16[32,16]{0,1:T(8,128)(2,1)S(1)}, bf16[32,384]{1,0:T(8,128)(2,1)S(1)}) all-reduce(bf16[32,16]{0,1:T(8,128)(2,1)S(1)} %bitcast.79, bf16[32,384]{1,0:T(8,128)(2,1)S(1)} %copy.89), channel_id=1, replica_groups=mesh['parts'=2,'rows'=4,'cols'=4] {'cols'}, use_global_device_ids=true, to_apply=%region_12.13 | all-reduce | flops 12800 | bytes 51200 | tf_op jit(solution)/shard_map/psum | solution.py:106
  53.4 0.1 copy.78
  53.5 0.1 div.39
  53.6 0.2 div.40
  53.7 0.2 reshape.110
  54.0 0.1 add.82
  54.0 1.0 %convolution_add_fusion.3 = f32[32,384]{1,0:T(8,128)} fusion(f32[32,384]{1,0:T(8,128)S(1)} %get-tuple-element.140, bf16[384,384]{1,0:T(8,128)(2,1)S(1)} %copy-done, bf16[32,384]{1,0:T(8,128)(2,1)S(1)} %multiply_convert_fusion.4, bf16[384,1536]{1,0:T(8,128)(2,1)S(1)} %copy-done.2, f32[32,384]{1,0:T(8,128)S(1)} %div.40, ...), kind=kOutput, calls=%fused_computation.36 | convolution fusion | flops 18972672 | bytes 786432 | tf_op jit(solution)/shard_map/dot_general | solution.py:113
  55.0 0.1 reshape.112
  55.1 0.1 copy.83
  55.2 0.2 reshape.111
  55.4 0.8 %add_add_fusion = f32[32,4,512]{2,1,0:T(4,128)} fusion(f32[32,4,512]{2,1,0:T(4,128)S(1)} %reshape.110, f32[32,4,512]{2,1,0:T(4,128)S(1)} %reshape.111, f32[512]{0:T(512)S(1)} %add.82), kind=kLoop, calls=%fused_computation.44 | loop fusion | flops 131072 | bytes 788480 | tf_op jit(solution)/shard_map/add | solution.py:123
  (55 shorter events, 0.3 us)
Async XLA Ops:
  0.6 53.4 %copy-start = (bf16[384,384]{1,0:T(8,128)(2,1)S(1)}, bf16[384,384]{1,0:T(8,128)(2,1)}, u32[]{:S(2)}) copy-start(bf16[384,384]{1,0:T(8,128)(2,1)} %param.29) | copy-start | bytes 884740
  0.7 1.4 %copy-start.1 = (bf16[128,1024]{1,0:T(8,128)(2,1)S(1)}, bf16[128,1024]{1,0:T(8,128)(2,1)}, u32[]{:S(2)}) copy-start(bf16[128,1024]{1,0:T(8,128)(2,1)} %get-tuple-element.250) | copy-start | bytes 786436 | tf_op jit(solution)/shard_map/while
  0.7 1.4 %copy-start.8 = (f32[128]{0:T(128)S(1)}, f32[128]{0:T(128)}, u32[]{:S(2)}) copy-start(f32[128]{0:T(128)} %get-tuple-element.249) | copy-start | bytes 1540 | tf_op jit(solution)/shard_map/while
  2.1 0.9 %copy-start.14 = (bf16[512,128]{1,0:T(8,128)(2,1)S(1)}, bf16[512,128]{1,0:T(8,128)(2,1)}, u32[]{:S(2)}) copy-start(bf16[512,128]{1,0:T(8,128)(2,1)} %get-tuple-element.251) | copy-start | bytes 393220 | tf_op jit(solution)/shard_map/while
  3.5 0.7 %copy-start.4 = (bf16[128,16]{0,1:T(8,128)(2,1)S(1)}, bf16[128,16]{0,1:T(8,128)(2,1)}, u32[]{:S(2)}) copy-start(bf16[128,16]{0,1:T(8,128)(2,1)} %get-tuple-element.253) | copy-start | bytes 12292 | tf_op jit(solution)/shard_map/while
  3.5 0.7 %copy-start.7 = (f32[128]{0:T(128)S(1)}, f32[128]{0:T(128)}, u32[]{:S(2)}) copy-start(f32[128]{0:T(128)} %get-tuple-element.252) | copy-start | bytes 1540 | tf_op jit(solution)/shard_map/while
  3.5 1.1 %copy-start.3 = (bf16[128,64]{0,1:T(8,128)(2,1)S(1)}, bf16[128,64]{0,1:T(8,128)(2,1)}, u32[]{:S(2)}) copy-start(bf16[128,64]{0,1:T(8,128)(2,1)} %get-tuple-element.254) | copy-start | bytes 49156 | tf_op jit(solution)/shard_map/while
  4.7 1.4 %copy-start.1 = (bf16[128,1024]{1,0:T(8,128)(2,1)S(1)}, bf16[128,1024]{1,0:T(8,128)(2,1)}, u32[]{:S(2)}) copy-start(bf16[128,1024]{1,0:T(8,128)(2,1)} %get-tuple-element.250) | copy-start | bytes 786436 | tf_op jit(solution)/shard_map/while
  4.8 1.4 %copy-start.8 = (f32[128]{0:T(128)S(1)}, f32[128]{0:T(128)}, u32[]{:S(2)}) copy-start(f32[128]{0:T(128)} %get-tuple-element.249) | copy-start | bytes 1540 | tf_op jit(solution)/shard_map/while
  6.1 0.9 %copy-start.14 = (bf16[512,128]{1,0:T(8,128)(2,1)S(1)}, bf16[512,128]{1,0:T(8,128)(2,1)}, u32[]{:S(2)}) copy-start(bf16[512,128]{1,0:T(8,128)(2,1)} %get-tuple-element.251) | copy-start | bytes 393220 | tf_op jit(solution)/shard_map/while
  7.5 0.7 %copy-start.4 = (bf16[128,16]{0,1:T(8,128)(2,1)S(1)}, bf16[128,16]{0,1:T(8,128)(2,1)}, u32[]{:S(2)}) copy-start(bf16[128,16]{0,1:T(8,128)(2,1)} %get-tuple-element.253) | copy-start | bytes 12292 | tf_op jit(solution)/shard_map/while
  7.5 0.7 %copy-start.7 = (f32[128]{0:T(128)S(1)}, f32[128]{0:T(128)}, u32[]{:S(2)}) copy-start(f32[128]{0:T(128)} %get-tuple-element.252) | copy-start | bytes 1540 | tf_op jit(solution)/shard_map/while
  7.5 1.1 %copy-start.3 = (bf16[128,64]{0,1:T(8,128)(2,1)S(1)}, bf16[128,64]{0,1:T(8,128)(2,1)}, u32[]{:S(2)}) copy-start(bf16[128,64]{0,1:T(8,128)(2,1)} %get-tuple-element.254) | copy-start | bytes 49156 | tf_op jit(solution)/shard_map/while
  8.8 9.4 %copy-start.13 = (f32[2,512,128]{2,1,0:T(8,128)}, f32[2,512,128]{2,1,0:T(8,128)S(1)}, u32[]{:S(2)}) copy-start(f32[2,512,128]{2,1,0:T(8,128)S(1)} %get-tuple-element.62) | copy-start | bytes 1572868
  8.8 8.5 %copy-start.5 = (f32[32,384]{1,0:T(8,128)S(1)}, f32[32,384]{1,0:T(8,128)}, u32[]{:S(2)}) copy-start(f32[32,384]{1,0:T(8,128)} %param.18) | copy-start | bytes 147460
  8.8 8.5 %copy-start.6 = (f32[32,384]{1,0:T(8,128)S(1)}, f32[32,384]{1,0:T(8,128)}, u32[]{:S(2)}) copy-start(f32[32,384]{1,0:T(8,128)} %param.26) | copy-start | bytes 147460
  8.8 8.5 %copy-start.11 = (s32[32]{0:T(128)S(1)}, s32[32]{0:T(128)}, u32[]{:S(2)}) copy-start(s32[32]{0:T(128)} %param.19) | copy-start | bytes 388
  8.8 9.3 %copy-start.9 = (f32[384]{0:T(512)S(1)}, f32[384]{0:T(512)}, u32[]{:S(2)}) copy-start(f32[384]{0:T(512)} %param.27) | copy-start | bytes 4612
  8.8 9.4 %copy-start.2 = (bf16[384,1536]{1,0:T(8,128)(2,1)S(1)}, bf16[384,1536]{1,0:T(8,128)(2,1)}, u32[]{:S(2)}) copy-start(bf16[384,1536]{1,0:T(8,128)(2,1)} %param.28) | copy-start | bytes 3538948
  9.9 45.1 %all-to-all-start = ((bf16[16,1,8,512]{3,2,1,0:T(8,128)(2,1)}), bf16[16,1,8,512]{3,2,1,0:T(8,128)(2,1)S(1)}, u32[]{:S(2)}, u32[]{:S(2)}) async-start(bf16[16,1,8,512]{3,2,1,0:T(8,128)(2,1)} %bitcast.16), calls=%async_computation | async-start | bytes 262144 | tf_op jit(solution)/shard_map/all_to_all | solution.py:118
  17.6 6.6 %copy-start.10 = (s32[4,4,1]{1,2,0:T(1,128)S(1)}, s32[4,4,1]{1,2,0:T(1,128)}, u32[]{:S(2)}) copy-start(s32[4,4,1]{1,2,0:T(1,128)} %param.20) | copy-start | bytes 196
  37.3 16.7 %copy-start.12 = (f32[64]{0:T(128)S(1)}, f32[64]{0:T(128)}, u32[]{:S(2)}) copy-start(f32[64]{0:T(128)} %param.31) | copy-start | bytes 772
where the time goes:
time: 56.6 us; the launch traced here: 56.2 us
  blocking collectives  33.3 us (59%)
  starting transfers between devices  7.39 us (13%)
  local copies, waits for them, and re-layouts  5.89 us (10%)
  matrix products  4.73 us (8%)
  other arithmetic  3.66 us (6%)
  between operations  0.96 us (2%)
    psum x1, blocking collectives, local(): lax.psum(totals.astype(jnp.bfloat16), 'cols').astype(jnp.float32)  15.8 us
    pmax x1, blocking collectives, local(): row_max = lax.pmax(local_max, 'cols')  12.1 us
    all_to_all x1, starting transfers between devices, local(): lax.all_to_all(outgoing, ('rows', 'cols'), split_axis=0, concat_axis=1, t...  7.39 us
    all_gather x1, blocking collectives, local(): key_values = lax.all_gather(local_kv, 'rows', axis=0, tiled=True)  5.33 us
    reduce_sum x2, other arithmetic, layer_norm(): average = jnp.mean(values, axis=-1, keepdims=True)  2.28 us
    while x24, local copies, waits for them, and re-layouts  1.65 us
  transfers between devices with their start and end apart: 1, of which 0 were waited for; matrix products, arithmetic and copies ran while one was open for 7% of the time, Pallas kernels for 0%

commit v1 on v0

--- a/solution.py
+++ b/solution.py
@@ -5,6 +5,18 @@
 from jax.sharding import PartitionSpec as P
 
 eps_norm = 1e-05
+
+
+def in_blocks(array, dim, size):
+    shape = array.shape
+    parts = array.reshape(*shape[:dim], size, shape[dim] // size, *shape[dim + 1 :])
+    return jnp.moveaxis(parts, dim, 0)
+
+
+def in_order(pieces, dim):
+    shape = list(pieces.shape[1:])
+    shape[dim] *= pieces.shape[0]
+    return jnp.moveaxis(pieces, 0, dim).reshape(shape)
 
 
 def layer_norm(values, gain_vec):
@@ -115,7 +127,17 @@
     outgoing = jnp.transpose(grouped, (2, 0, 1, 3)).reshape(
         key_groups * q_groups, 1, block_len, block_len * bin_count
     )
-    arrived = lax.all_to_all(outgoing, ("rows", "cols"), split_axis=0, concat_axis=1, tiled=True)
+    count, mine = (lax.axis_size(("rows", "cols")), lax.axis_index(("rows", "cols")))
+    parts = in_blocks(outgoing, 0, count)
+    filled = parts
+    for step in range(1, count):
+        target, source = ((mine + step) % count, (mine - step) % count)
+        sent = lax.dynamic_index_in_dim(parts, target, 0)
+        partner_block = lax.ppermute(
+            sent, ("rows", "cols"), [(i, (i + step) % count) for i in range(count)]
+        )
+        filled = lax.dynamic_update_slice_in_dim(filled, partner_block, source, axis=0)
+    arrived = in_order(filled, 1)
     mirrored = jnp.transpose(
         arrived.reshape(key_groups, q_groups, block_len, block_len, bin_count), (1, 3, 0, 2, 4)
     )

time: 56.6 us -> 73 us (1.29)
  starting transfers between devices: 7.39 us -> 21.9 us
  waiting for transfers between devices: 0.01 us -> 2.11 us
    ppermute x0 -> x15, starting transfers between devices: none -> 21.9 us  [local(): lax.ppermute(sent, ('rows', 'cols'), [(i, (i + step) % count) for i in ra...]
    all_to_all x1 -> x0, starting transfers between devices: 7.39 us -> none  [local(): lax.all_to_all(outgoing, ('rows', 'cols'), split_axis=0, concat_axis=1, t...]
    ppermute x0 -> x15, waiting for transfers between devices: none -> 2.11 us  [local(): lax.ppermute(sent, ('rows', 'cols'), [(i, (i + step) % count) for i in ra...]
    psum x1, blocking collectives: 15.8 us -> 17.5 us  [local(): lax.psum(weighted.astype(jnp.bfloat16), 'cols').astype(jnp.float32)]
    pmax x1, blocking collectives: 12.1 us -> 10.6 us  [local(): row_max = lax.pmax(local_max, 'cols')]
    dynamic_update_slice x8, local copies, waits for them, and re-layouts: 0.69 us -> 2.09 us  [local(): updated, head_bias, binned = lax.map(run_tile, pair_tiles)]
    while x24, local copies, waits for them, and re-layouts: 1.65 us -> 0.81 us
  transfers between devices with their start and end apart: 1 -> 15, of which waited for: 0 -> 2; matrix products, arithmetic and copies ran while one was open for 7% -> 5% of each run, Pallas kernels for 0% -> 0%
where the time goes in v1:
time: 73 us; the launch traced here: 72.7 us
  blocking collectives  33.3 us (46%)
  starting transfers between devices  21.9 us (30%)
  local copies, waits for them, and re-layouts  5.4 us (7%)
  matrix products  4.9 us (7%)
  other arithmetic  3.69 us (5%)
  waiting for transfers between devices  2.11 us (3%)
  between operations  1.17 us (2%)
    ppermute x15, starting transfers between devices, local(): lax.ppermute(sent, ('rows', 'cols'), [(i, (i + step) % count) for i in ra...  21.9 us
    psum x1, blocking collectives, local(): lax.psum(weighted.astype(jnp.bfloat16), 'cols').astype(jnp.float32)  17.5 us
    pmax x1, blocking collectives, local(): row_max = lax.pmax(local_max, 'cols')  10.6 us
    all_gather x1, blocking collectives, local(): key_values = lax.all_gather(local_kv, 'rows', axis=0, tiled=True)  5.24 us
    reduce_sum x2, other arithmetic, layer_norm(): average = jnp.mean(values, axis=-1, keepdims=True)  2.28 us
    ppermute x15, waiting for transfers between devices, local(): lax.ppermute(sent, ('rows', 'cols'), [(i, (i + step) % count) for i in ra...  2.11 us
    dynamic_update_slice x8, local copies, waits for them, and re-layouts, local(): updated, head_bias, binned = lax.map(run_tile, pair_tiles)  2.09 us
  transfers between devices with their start and end apart: 15, of which 2 were waited for; matrix products, arithmetic and copies ran while one was open for 5% of the time, Pallas kernels for 0%

profile of v1, /device:TPU:0, one launch (start us, length us, event | category | flops | bytes accessed | tf_op | source)
XLA Modules:
  0.0 72.7 jit_solution(141157663400018448)
XLA Ops:
  0.7 8.7 %while.14 = (s32[]{:T(128)}, f32[2,512,128]{2,1,0:T(8,128)}, f32[2,512,16]{1,0,2:T(2,128)S(1)}, bf16[2,512,64]{1,2,0:T(8,128)(2,1)S(1)}, f32[2,512,128]{2,1,0:T(...) while((s32[]{:T(128)}, f32[2,512,128]{2,1,0:T(8,128)}, ...), condition=%wide.region_5.6_spmd, body=%wide.region_0.5_spmd.sunk | while | flops 214598656 | bytes 10466621 | solution.py:75
  0.7 1.1 %fusion.63 = (f32[512]{0:T(512)S(1)}, f32[1,512,128]{2,1,0:T(8,128)S(1)}) fusion(f32[2,512,128]{2,1,0:T(8,128)} %get-tuple-element.230, s32[]{:T(128)S(6)} %copy.65), kind=kLoop, calls=%fused_computation.92.clone.1 | loop fusion | flops 65024 | bytes 526340 | tf_op jit(solution)/shard_map/while/body/eval_jaxpr/reduce_sum | solution.py:23
  1.9 0.1 copy.55
  2.1 0.5 fusion.64
  2.6 0.4 copy-done.13
  3.0 0.5 fusion.65
  3.5 0.1 copy.56
  3.6 0.7 constant_dynamic-update-slice_fusion.17
  4.4 0.2 convolution_bitcast_fusion.2
  4.7 0.2 dynamic_update_slice.94
  4.9 0.2 fusion.66
  5.1 1.1 %fusion.63 = (f32[512]{0:T(512)S(1)}, f32[1,512,128]{2,1,0:T(8,128)S(1)}) fusion(f32[2,512,128]{2,1,0:T(8,128)} %get-tuple-element.230, s32[]{:T(128)S(6)} %copy.65), kind=kLoop, calls=%fused_computation.92.clone.1 | loop fusion | flops 65024 | bytes 526340 | tf_op jit(solution)/shard_map/while/body/eval_jaxpr/reduce_sum | solution.py:23
  6.2 0.1 copy.55
  6.5 0.5 fusion.64
  7.0 0.4 copy-done.13
  7.3 0.5 fusion.65
  7.8 0.1 copy.56
  8.0 0.7 constant_dynamic-update-slice_fusion.17
  8.8 0.2 convolution_bitcast_fusion.2
  9.0 0.2 dynamic_update_slice.94
  9.2 0.2 fusion.66
  9.4 0.2 copy.35
  9.6 0.2 reshape_reshape.6
  9.8 3.1 %collective-permute-start = (bf16[1,1,1,8,512]{4,3,0,2,1:T(8,128)(2,1)S(1)}, bf16[1,1,1,8,512]{4,3,0,2,1:T(8,128)(2,1)S(1)}, u32[]{:S(2)}, u32[]{:S(2)}) collective-permute-start(bf16[1,1,1,8,512]{4,3,0,2,1:T(8,128)(2,1)S(1)} %constant_dynamic-slice_fusion.15), channel_id=1, source_target_pairs={{0,1},{1,2},{2,3},{3,4},{4,5},{5,6},{6,7},{7,8},{8,9},{9,10},{10,1... | collective-permute-start | bytes 24584 | tf_op jit(solution)/shard_map/ppermute | solution.py:136
  12.9 0.1 copy.34
  13.2 0.3 fusion.36
  13.6 0.2 multiply_reduce_fusion.2
  13.8 0.1 multiply_convert_fusion.4
  13.9 0.2 fusion.21
  14.0 0.2 convolution_convert_fusion.2
  14.2 5.2 %all_gather.3 = bf16[32,768]{1,0:T(8,128)(2,1)S(1)} all-gather(bf16[8,768]{1,0:T(8,128)(2,1)S(1)} %convolution_convert_fusion.2), channel_id=1, replica_groups=mesh['parts'=2,'rows'=4,'cols'=4] {'rows'}, dimensions={0}, use_global_device_ids=true | all-gather | bytes 61440 | tf_op jit(solution)/shard_map/all_gather | solution.py:97
  19.5 0.1 copy.39
  19.6 0.1 reshape.100
  19.7 0.1 copy.31
  19.9 0.1 copy.41
  20.0 0.1 copy.42
  20.1 0.1 copy.40
  20.3 0.1 broadcast_in_dim.41
  20.3 0.1 gt.20
  20.4 0.3 fusion.37
  20.7 10.6 %pmax.7 = f32[16,32]{1,0:T(8,128)S(1)} all-reduce(f32[16,32]{1,0:T(8,128)S(1)} %get-tuple-element.123), channel_id=1, replica_groups=mesh['parts'=2,'rows'=4,'cols'=4] {'cols'}, use_global_device_ids=true, to_apply=%region_9.10 | all-reduce | flops 512 | bytes 4096 | tf_op jit(solution)/shard_map/pmax | solution.py:111
  31.4 0.2 convolution_convert_fusion.1
  31.6 17.5 %all-reduce = (bf16[32,384]{0,1:T(8,128)(2,1)S(1)}, bf16[32,16]{0,1:T(8,128)(2,1)S(1)}) all-reduce(bf16[32,384]{0,1:T(8,128)(2,1)S(1)} %bitcast.80, bf16[32,16]{0,1:T(8,128)(2,1)S(1)} %bitcast.83), channel_id=1, replica_groups=mesh['parts'=2,'rows'=4,'cols'=4] {'cols'}, use_global_device_ids=true, to_apply=%region_10.11 | all-reduce | flops 12800 | bytes 51200 | tf_op jit(solution)/shard_map/psum | solution.py:119
  49.1 1.1 %fusion.20 = f32[32,384]{1,0:T(8,128)} fusion(f32[32,384]{1,0:T(8,128)S(1)} %get-tuple-element.122, bf16[384,384]{1,0:T(8,128)(2,1)S(1)} %copy-done, f32[32,384]{0,1:T(8,128)S(1)} %bitcast_divide_fusion, bf16[32,384]{1,0:T(8,128)(2,1)S(1)} %multiply_convert_fusion.4, bf16[384,1536]{1,0:T(8,128)(2,1)S(1)} %copy-done.2), kind=kOutput, calls=%fused_computation.37 | convolution fusion | flops 18948096 | bytes 909312 | tf_op jit(solution)/shard_map/dot_general | solution.py:125
  50.3 0.7 %collective-permute-start.1 = (bf16[1,1,1,8,512]{4,3,0,2,1:T(8,128)(2,1)S(1)}, bf16[1,1,1,8,512]{4,3,0,2,1:T(8,128)(2,1)S(1)}, u32[]{:S(2)}, u32[]{:S(2)}) collective-permute-start(bf16[1,1,1,8,512]{4,3,0,2,1:T(8,128)(2,1)S(1)} %get-tuple-element.117), channel_id=1, source_target_pairs={{0,2},{1,3},{2,4},{3,5},{4,6},{5,7},{6,8},{7,9},{8,10},{9,11},{10,... | collective-permute-start | bytes 24584 | tf_op jit(solution)/shard_map/ppermute | solution.py:136
  51.0 0.2 reshape.101
  51.3 1.5 %collective-permute-start.2 = (bf16[1,1,1,8,512]{4,3,0,2,1:T(8,128)(2,1)S(1)}, bf16[1,1,1,8,512]{4,3,0,2,1:T(8,128)(2,1)S(1)}, u32[]{:S(2)}, u32[]{:S(2)}) collective-permute-start(bf16[1,1,1,8,512]{4,3,0,2,1:T(8,128)(2,1)S(1)} %get-tuple-element.116), channel_id=1, source_target_pairs={{0,3},{1,4},{2,5},{3,6},{4,7},{5,8},{6,9},{7,10},{8,11},{9,12},{10... | collective-permute-start | bytes 24584 | tf_op jit(solution)/shard_map/ppermute | solution.py:136
  52.8 1.0 %collective-permute-start.3 = (bf16[1,1,1,8,512]{4,3,0,2,1:T(8,128)(2,1)S(1)}, bf16[1,1,1,8,512]{4,3,0,2,1:T(8,128)(2,1)S(1)}, u32[]{:S(2)}, u32[]{:S(2)}) collective-permute-start(bf16[1,1,1,8,512]{4,3,0,2,1:T(8,128)(2,1)S(1)} %get-tuple-element.115), channel_id=1, source_target_pairs={{0,4},{1,5},{2,6},{3,7},{4,8},{5,9},{6,10},{7,11},{8,12},{9,13},{1... | collective-permute-start | bytes 24584 | tf_op jit(solution)/shard_map/ppermute | solution.py:136
  53.8 0.6 collective-permute-start.4
  54.4 1.6 %collective-permute-start.5 = (bf16[1,1,1,8,512]{4,3,0,2,1:T(8,128)(2,1)S(1)}, bf16[1,1,1,8,512]{4,3,0,2,1:T(8,128)(2,1)S(1)}, u32[]{:S(2)}, u32[]{:S(2)}) collective-permute-start(bf16[1,1,1,8,512]{4,3,0,2,1:T(8,128)(2,1)S(1)} %get-tuple-element.113), channel_id=1, source_target_pairs={{0,6},{1,7},{2,8},{3,9},{4,10},{5,11},{6,12},{7,13},{8,14},{9,15},... | collective-permute-start | bytes 24584 | tf_op jit(solution)/shard_map/ppermute | solution.py:136
  56.0 2.9 %collective-permute-start.6 = (bf16[1,1,1,8,512]{4,3,0,2,1:T(8,128)(2,1)S(1)}, bf16[1,1,1,8,512]{4,3,0,2,1:T(8,128)(2,1)S(1)}, u32[]{:S(2)}, u32[]{:S(2)}) collective-permute-start(bf16[1,1,1,8,512]{4,3,0,2,1:T(8,128)(2,1)S(1)} %get-tuple-element.112), channel_id=1, source_target_pairs={{0,7},{1,8},{2,9},{3,10},{4,11},{5,12},{6,13},{7,14},{8,15},{9,0},... | collective-permute-start | bytes 24584 | tf_op jit(solution)/shard_map/ppermute | solution.py:136
  58.9 0.5 collective-permute-start.7
  59.5 1.0 %collective-permute-start.8 = (bf16[1,1,1,8,512]{4,3,0,2,1:T(8,128)(2,1)S(1)}, bf16[1,1,1,8,512]{4,3,0,2,1:T(8,128)(2,1)S(1)}, u32[]{:S(2)}, u32[]{:S(2)}) collective-permute-start(bf16[1,1,1,8,512]{4,3,0,2,1:T(8,128)(2,1)S(1)} %get-tuple-element.110), channel_id=1, source_target_pairs={{0,9},{1,10},{2,11},{3,12},{4,13},{5,14},{6,15},{7,0},{8,1},{9,2},... | collective-permute-start | bytes 24584 | tf_op jit(solution)/shard_map/ppermute | solution.py:136
  60.4 1.6 %collective-permute-start.9 = (bf16[1,1,1,8,512]{4,3,0,2,1:T(8,128)(2,1)S(1)}, bf16[1,1,1,8,512]{4,3,0,2,1:T(8,128)(2,1)S(1)}, u32[]{:S(2)}, u32[]{:S(2)}) collective-permute-start(bf16[1,1,1,8,512]{4,3,0,2,1:T(8,128)(2,1)S(1)} %get-tuple-element.109), channel_id=1, source_target_pairs={{0,10},{1,11},{2,12},{3,13},{4,14},{5,15},{6,0},{7,1},{8,2},{9,3},... | collective-permute-start | bytes 24584 | tf_op jit(solution)/shard_map/ppermute | solution.py:136
  62.0 2.7 %collective-permute-start.10 = (bf16[1,1,1,8,512]{4,3,0,2,1:T(8,128)(2,1)S(1)}, bf16[1,1,1,8,512]{4,3,0,2,1:T(8,128)(2,1)S(1)}, u32[]{:S(2)}, u32[]{:S(2)}) collective-permute-start(bf16[1,1,1,8,512]{4,3,0,2,1:T(8,128)(2,1)S(1)} %get-tuple-element.108), channel_id=1, source_target_pairs={{0,11},{1,12},{2,13},{3,14},{4,15},{5,0},{6,1},{7,2},{8,3},{9,4},{... | collective-permute-start | bytes 24584 | tf_op jit(solution)/shard_map/ppermute | solution.py:136
  64.7 1.1 %collective-permute-start.11 = (bf16[1,1,1,8,512]{4,3,0,2,1:T(8,128)(2,1)S(1)}, bf16[1,1,1,8,512]{4,3,0,2,1:T(8,128)(2,1)S(1)}, u32[]{:S(2)}, u32[]{:S(2)}) collective-permute-start(bf16[1,1,1,8,512]{4,3,0,2,1:T(8,128)(2,1)S(1)} %get-tuple-element.107), channel_id=1, source_target_pairs={{0,12},{1,13},{2,14},{3,15},{4,0},{5,1},{6,2},{7,3},{8,4},{9,5},{1... | collective-permute-start | bytes 24584 | tf_op jit(solution)/shard_map/ppermute | solution.py:136
  65.8 1.0 %collective-permute-start.13 = (bf16[1,1,1,8,512]{4,3,0,2,1:T(8,128)(2,1)S(1)}, bf16[1,1,1,8,512]{4,3,0,2,1:T(8,128)(2,1)S(1)}, u32[]{:S(2)}, u32[]{:S(2)}) collective-permute-start(bf16[1,1,1,8,512]{4,3,0,2,1:T(8,128)(2,1)S(1)} %get-tuple-element.105), channel_id=1, source_target_pairs={{0,14},{1,15},{2,0},{3,1},{4,2},{5,3},{6,4},{7,5},{8,6},{9,7},{10,... | collective-permute-start | bytes 24584 | tf_op jit(solution)/shard_map/ppermute | solution.py:136
  66.8 2.6 %collective-permute-start.14 = (bf16[1,1,1,8,512]{4,3,0,2,1:T(8,128)(2,1)S(1)}, bf16[1,1,1,8,512]{4,3,0,2,1:T(8,128)(2,1)S(1)}, u32[]{:S(2)}, u32[]{:S(2)}) collective-permute-start(bf16[1,1,1,8,512]{4,3,0,2,1:T(8,128)(2,1)S(1)} %get-tuple-element.104), channel_id=1, source_target_pairs={{0,15},{1,0},{2,1},{3,2},{4,3},{5,4},{6,5},{7,6},{8,7},{9,8},{10,9... | collective-permute-start | bytes 24584 | tf_op jit(solution)/shard_map/ppermute | solution.py:136
  69.4 1.8 %collective-permute-done.12 = bf16[1,1,1,8,512]{4,3,0,2,1:T(8,128)(2,1)S(1)} collective-permute-done((bf16[1,1,1,8,512]{4,3,0,2,1:T(8,128)(2,1)S(1)}, bf16[1,1,1,8,512]{4,3,0,2,1:T(8,128)(2,1)S(1)}, u32[]{:S(2)}, u32[]{:S(2)}) %collective-permute-start.12) | collective-permute-done | bytes 8224 | tf_op jit(solution)/shard_map/ppermute | solution.py:136
  71.2 0.3 collective-permute-done.14
  71.5 0.1 reshape.103
  71.7 0.1 copy.37
  71.8 0.2 reshape.102
  72.0 0.8 %add_add_fusion = f32[32,4,512]{2,1,0:T(4,128)} fusion(f32[32,4,512]{2,1,0:T(4,128)S(1)} %reshape.101, f32[32,4,512]{2,1,0:T(4,128)S(1)} %reshape.102, f32[512]{0:T(512)S(1)} %add.403), kind=kLoop, calls=%fused_computation.45 | loop fusion | flops 131072 | bytes 788480 | tf_op jit(solution)/shard_map/add | solution.py:145
  (95 shorter events, 0.8 us)
Async XLA Ops:
  0.6 48.5 %copy-start = (bf16[384,384]{1,0:T(8,128)(2,1)S(1)}, bf16[384,384]{1,0:T(8,128)(2,1)}, u32[]{:S(2)}) copy-start(bf16[384,384]{1,0:T(8,128)(2,1)} %param.29) | copy-start | bytes 884740
  0.7 1.4 %copy-start.1 = (bf16[128,1024]{1,0:T(8,128)(2,1)S(1)}, bf16[128,1024]{1,0:T(8,128)(2,1)}, u32[]{:S(2)}) copy-start(bf16[128,1024]{1,0:T(8,128)(2,1)} %get-tuple-element.232) | copy-start | bytes 786436 | tf_op jit(solution)/shard_map/while
  0.7 1.4 %copy-start.8 = (f32[128]{0:T(128)S(1)}, f32[128]{0:T(128)}, u32[]{:S(2)}) copy-start(f32[128]{0:T(128)} %get-tuple-element.231) | copy-start | bytes 1540 | tf_op jit(solution)/shard_map/while
  2.1 0.9 %copy-start.13 = (bf16[512,128]{1,0:T(8,128)(2,1)S(1)}, bf16[512,128]{1,0:T(8,128)(2,1)}, u32[]{:S(2)}) copy-start(bf16[512,128]{1,0:T(8,128)(2,1)} %get-tuple-element.233) | copy-start | bytes 393220 | tf_op jit(solution)/shard_map/while
  3.5 1.0 %copy-start.4 = (bf16[128,16]{0,1:T(8,128)(2,1)S(1)}, bf16[128,16]{0,1:T(8,128)(2,1)}, u32[]{:S(2)}) copy-start(bf16[128,16]{0,1:T(8,128)(2,1)} %get-tuple-element.235) | copy-start | bytes 12292 | tf_op jit(solution)/shard_map/while
  3.5 1.0 %copy-start.7 = (f32[128]{0:T(128)S(1)}, f32[128]{0:T(128)}, u32[]{:S(2)}) copy-start(f32[128]{0:T(128)} %get-tuple-element.234) | copy-start | bytes 1540 | tf_op jit(solution)/shard_map/while
  3.5 1.4 %copy-start.3 = (bf16[128,64]{0,1:T(8,128)(2,1)S(1)}, bf16[128,64]{0,1:T(8,128)(2,1)}, u32[]{:S(2)}) copy-start(bf16[128,64]{0,1:T(8,128)(2,1)} %get-tuple-element.236) | copy-start | bytes 49156 | tf_op jit(solution)/shard_map/while
  5.0 1.4 %copy-start.1 = (bf16[128,1024]{1,0:T(8,128)(2,1)S(1)}, bf16[128,1024]{1,0:T(8,128)(2,1)}, u32[]{:S(2)}) copy-start(bf16[128,1024]{1,0:T(8,128)(2,1)} %get-tuple-element.232) | copy-start | bytes 786436 | tf_op jit(solution)/shard_map/while
  5.1 1.4 %copy-start.8 = (f32[128]{0:T(128)S(1)}, f32[128]{0:T(128)}, u32[]{:S(2)}) copy-start(f32[128]{0:T(128)} %get-tuple-element.231) | copy-start | bytes 1540 | tf_op jit(solution)/shard_map/while
  6.4 0.9 %copy-start.13 = (bf16[512,128]{1,0:T(8,128)(2,1)S(1)}, bf16[512,128]{1,0:T(8,128)(2,1)}, u32[]{:S(2)}) copy-start(bf16[512,128]{1,0:T(8,128)(2,1)} %get-tuple-element.233) | copy-start | bytes 393220 | tf_op jit(solution)/shard_map/while
  7.8 1.0 %copy-start.4 = (bf16[128,16]{0,1:T(8,128)(2,1)S(1)}, bf16[128,16]{0,1:T(8,128)(2,1)}, u32[]{:S(2)}) copy-start(bf16[128,16]{0,1:T(8,128)(2,1)} %get-tuple-element.235) | copy-start | bytes 12292 | tf_op jit(solution)/shard_map/while
  7.8 1.0 %copy-start.7 = (f32[128]{0:T(128)S(1)}, f32[128]{0:T(128)}, u32[]{:S(2)}) copy-start(f32[128]{0:T(128)} %get-tuple-element.234) | copy-start | bytes 1540 | tf_op jit(solution)/shard_map/while
  7.8 1.4 %copy-start.3 = (bf16[128,64]{0,1:T(8,128)(2,1)S(1)}, bf16[128,64]{0,1:T(8,128)(2,1)}, u32[]{:S(2)}) copy-start(bf16[128,64]{0,1:T(8,128)(2,1)} %get-tuple-element.236) | copy-start | bytes 49156 | tf_op jit(solution)/shard_map/while
  9.4 3.8 %copy-start.5 = (f32[32,384]{1,0:T(8,128)S(1)}, f32[32,384]{1,0:T(8,128)}, u32[]{:S(2)}) copy-start(f32[32,384]{1,0:T(8,128)} %param.18) | copy-start | bytes 147460
  9.4 3.8 %copy-start.6 = (f32[32,384]{1,0:T(8,128)S(1)}, f32[32,384]{1,0:T(8,128)}, u32[]{:S(2)}) copy-start(f32[32,384]{1,0:T(8,128)} %param.26) | copy-start | bytes 147460
  9.4 3.8 %copy-start.11 = (s32[32]{0:T(128)S(1)}, s32[32]{0:T(128)}, u32[]{:S(2)}) copy-start(s32[32]{0:T(128)} %param.19) | copy-start | bytes 388
  9.4 4.3 %copy-start.9 = (f32[384]{0:T(512)S(1)}, f32[384]{0:T(512)}, u32[]{:S(2)}) copy-start(f32[384]{0:T(512)} %param.27) | copy-start | bytes 4612
  9.4 4.4 %copy-start.2 = (bf16[384,1536]{1,0:T(8,128)(2,1)S(1)}, bf16[384,1536]{1,0:T(8,128)(2,1)}, u32[]{:S(2)}) copy-start(bf16[384,1536]{1,0:T(8,128)(2,1)} %param.28) | copy-start | bytes 3538948
  9.8 40.4 %collective-permute-start = (bf16[1,1,1,8,512]{4,3,0,2,1:T(8,128)(2,1)S(1)}, bf16[1,1,1,8,512]{4,3,0,2,1:T(8,128)(2,1)S(1)}, u32[]{:S(2)}, u32[]{:S(2)}) collective-permute-start(bf16[1,1,1,8,512]{4,3,0,2,1:T(8,128)(2,1)S(1)} %constant_dynamic-slice_fusion.15), channel_id=1, source_target_pairs={{0,1},{1,2},{2,3},{3,4},{4,5},{5,6},{6,7},{7,8},{8,9},{9,10},{10,1... | collective-permute-start | bytes 24584 | tf_op jit(solution)/shard_map/ppermute | solution.py:136
  13.8 6.3 %copy-start.10 = (s32[4,4,1]{1,2,0:T(1,128)S(1)}, s32[4,4,1]{1,2,0:T(1,128)}, u32[]{:S(2)}) copy-start(s32[4,4,1]{1,2,0:T(1,128)} %param.20) | copy-start | bytes 196
  49.1 2.1 %copy-start.12 = (f32[64]{0:T(128)S(1)}, f32[64]{0:T(128)}, u32[]{:S(2)}) copy-start(f32[64]{0:T(128)} %param.31) | copy-start | bytes 772
  50.3 5.7 %collective-permute-start.1 = (bf16[1,1,1,8,512]{4,3,0,2,1:T(8,128)(2,1)S(1)}, bf16[1,1,1,8,512]{4,3,0,2,1:T(8,128)(2,1)S(1)}, u32[]{:S(2)}, u32[]{:S(2)}) collective-permute-start(bf16[1,1,1,8,512]{4,3,0,2,1:T(8,128)(2,1)S(1)} %get-tuple-element.117), channel_id=1, source_target_pairs={{0,2},{1,3},{2,4},{3,5},{4,6},{5,7},{6,8},{7,9},{8,10},{9,11},{10,... | collective-permute-start | bytes 24584 | tf_op jit(solution)/shard_map/ppermute | solution.py:136
  51.3 7.6 %collective-permute-start.2 = (bf16[1,1,1,8,512]{4,3,0,2,1:T(8,128)(2,1)S(1)}, bf16[1,1,1,8,512]{4,3,0,2,1:T(8,128)(2,1)S(1)}, u32[]{:S(2)}, u32[]{:S(2)}) collective-permute-start(bf16[1,1,1,8,512]{4,3,0,2,1:T(8,128)(2,1)S(1)} %get-tuple-element.116), channel_id=1, source_target_pairs={{0,3},{1,4},{2,5},{3,6},{4,7},{5,8},{6,9},{7,10},{8,11},{9,12},{10... | collective-permute-start | bytes 24584 | tf_op jit(solution)/shard_map/ppermute | solution.py:136
  52.8 6.7 %collective-permute-start.3 = (bf16[1,1,1,8,512]{4,3,0,2,1:T(8,128)(2,1)S(1)}, bf16[1,1,1,8,512]{4,3,0,2,1:T(8,128)(2,1)S(1)}, u32[]{:S(2)}, u32[]{:S(2)}) collective-permute-start(bf16[1,1,1,8,512]{4,3,0,2,1:T(8,128)(2,1)S(1)} %get-tuple-element.115), channel_id=1, source_target_pairs={{0,4},{1,5},{2,6},{3,7},{4,8},{5,9},{6,10},{7,11},{8,12},{9,13},{1... | collective-permute-start | bytes 24584 | tf_op jit(solution)/shard_map/ppermute | solution.py:136
  53.8 6.6 %collective-permute-start.4 = (bf16[1,1,1,8,512]{4,3,0,2,1:T(8,128)(2,1)S(1)}, bf16[1,1,1,8,512]{4,3,0,2,1:T(8,128)(2,1)S(1)}, u32[]{:S(2)}, u32[]{:S(2)}) collective-permute-start(bf16[1,1,1,8,512]{4,3,0,2,1:T(8,128)(2,1)S(1)} %get-tuple-element.114), channel_id=1, source_target_pairs={{0,5},{1,6},{2,7},{3,8},{4,9},{5,10},{6,11},{7,12},{8,13},{9,14},{... | collective-permute-start | bytes 24584 | tf_op jit(solution)/shard_map/ppermute | solution.py:136
  54.4 7.6 %collective-permute-start.5 = (bf16[1,1,1,8,512]{4,3,0,2,1:T(8,128)(2,1)S(1)}, bf16[1,1,1,8,512]{4,3,0,2,1:T(8,128)(2,1)S(1)}, u32[]{:S(2)}, u32[]{:S(2)}) collective-permute-start(bf16[1,1,1,8,512]{4,3,0,2,1:T(8,128)(2,1)S(1)} %get-tuple-element.113), channel_id=1, source_target_pairs={{0,6},{1,7},{2,8},{3,9},{4,10},{5,11},{6,12},{7,13},{8,14},{9,15},... | collective-permute-start | bytes 24584 | tf_op jit(solution)/shard_map/ppermute | solution.py:136
  56.0 8.7 %collective-permute-start.6 = (bf16[1,1,1,8,512]{4,3,0,2,1:T(8,128)(2,1)S(1)}, bf16[1,1,1,8,512]{4,3,0,2,1:T(8,128)(2,1)S(1)}, u32[]{:S(2)}, u32[]{:S(2)}) collective-permute-start(bf16[1,1,1,8,512]{4,3,0,2,1:T(8,128)(2,1)S(1)} %get-tuple-element.112), channel_id=1, source_target_pairs={{0,7},{1,8},{2,9},{3,10},{4,11},{5,12},{6,13},{7,14},{8,15},{9,0},... | collective-permute-start | bytes 24584 | tf_op jit(solution)/shard_map/ppermute | solution.py:136
  58.9 6.9 %collective-permute-start.7 = (bf16[1,1,1,8,512]{4,3,0,2,1:T(8,128)(2,1)S(1)}, bf16[1,1,1,8,512]{4,3,0,2,1:T(8,128)(2,1)S(1)}, u32[]{:S(2)}, u32[]{:S(2)}) collective-permute-start(bf16[1,1,1,8,512]{4,3,0,2,1:T(8,128)(2,1)S(1)} %get-tuple-element.111), channel_id=1, source_target_pairs={{0,8},{1,9},{2,10},{3,11},{4,12},{5,13},{6,14},{7,15},{8,0},{9,1},... | collective-permute-start | bytes 24584 | tf_op jit(solution)/shard_map/ppermute | solution.py:136
  59.5 6.3 %collective-permute-start.8 = (bf16[1,1,1,8,512]{4,3,0,2,1:T(8,128)(2,1)S(1)}, bf16[1,1,1,8,512]{4,3,0,2,1:T(8,128)(2,1)S(1)}, u32[]{:S(2)}, u32[]{:S(2)}) collective-permute-start(bf16[1,1,1,8,512]{4,3,0,2,1:T(8,128)(2,1)S(1)} %get-tuple-element.110), channel_id=1, source_target_pairs={{0,9},{1,10},{2,11},{3,12},{4,13},{5,14},{6,15},{7,0},{8,1},{9,2},... | collective-permute-start | bytes 24584 | tf_op jit(solution)/shard_map/ppermute | solution.py:136
  60.4 6.4 %collective-permute-start.9 = (bf16[1,1,1,8,512]{4,3,0,2,1:T(8,128)(2,1)S(1)}, bf16[1,1,1,8,512]{4,3,0,2,1:T(8,128)(2,1)S(1)}, u32[]{:S(2)}, u32[]{:S(2)}) collective-permute-start(bf16[1,1,1,8,512]{4,3,0,2,1:T(8,128)(2,1)S(1)} %get-tuple-element.109), channel_id=1, source_target_pairs={{0,10},{1,11},{2,12},{3,13},{4,14},{5,15},{6,0},{7,1},{8,2},{9,3},... | collective-permute-start | bytes 24584 | tf_op jit(solution)/shard_map/ppermute | solution.py:136
  62.0 7.4 %collective-permute-start.10 = (bf16[1,1,1,8,512]{4,3,0,2,1:T(8,128)(2,1)S(1)}, bf16[1,1,1,8,512]{4,3,0,2,1:T(8,128)(2,1)S(1)}, u32[]{:S(2)}, u32[]{:S(2)}) collective-permute-start(bf16[1,1,1,8,512]{4,3,0,2,1:T(8,128)(2,1)S(1)} %get-tuple-element.108), channel_id=1, source_target_pairs={{0,11},{1,12},{2,13},{3,14},{4,15},{5,0},{6,1},{7,2},{8,3},{9,4},{... | collective-permute-start | bytes 24584 | tf_op jit(solution)/shard_map/ppermute | solution.py:136
  64.7 4.7 %collective-permute-start.11 = (bf16[1,1,1,8,512]{4,3,0,2,1:T(8,128)(2,1)S(1)}, bf16[1,1,1,8,512]{4,3,0,2,1:T(8,128)(2,1)S(1)}, u32[]{:S(2)}, u32[]{:S(2)}) collective-permute-start(bf16[1,1,1,8,512]{4,3,0,2,1:T(8,128)(2,1)S(1)} %get-tuple-element.107), channel_id=1, source_target_pairs={{0,12},{1,13},{2,14},{3,15},{4,0},{5,1},{6,2},{7,3},{8,4},{9,5},{1... | collective-permute-start | bytes 24584 | tf_op jit(solution)/shard_map/ppermute | solution.py:136
  65.8 5.5 %collective-permute-start.12 = (bf16[1,1,1,8,512]{4,3,0,2,1:T(8,128)(2,1)S(1)}, bf16[1,1,1,8,512]{4,3,0,2,1:T(8,128)(2,1)S(1)}, u32[]{:S(2)}, u32[]{:S(2)}) collective-permute-start(bf16[1,1,1,8,512]{4,3,0,2,1:T(8,128)(2,1)S(1)} %get-tuple-element.106), channel_id=1, source_target_pairs={{0,13},{1,14},{2,15},{3,0},{4,1},{5,2},{6,3},{7,4},{8,5},{9,6},{10... | collective-permute-start | bytes 24584 | tf_op jit(solution)/shard_map/ppermute | solution.py:136
  65.8 5.4 %collective-permute-start.13 = (bf16[1,1,1,8,512]{4,3,0,2,1:T(8,128)(2,1)S(1)}, bf16[1,1,1,8,512]{4,3,0,2,1:T(8,128)(2,1)S(1)}, u32[]{:S(2)}, u32[]{:S(2)}) collective-permute-start(bf16[1,1,1,8,512]{4,3,0,2,1:T(8,128)(2,1)S(1)} %get-tuple-element.105), channel_id=1, source_target_pairs={{0,14},{1,15},{2,0},{3,1},{4,2},{5,3},{6,4},{7,5},{8,6},{9,7},{10,... | collective-permute-start | bytes 24584 | tf_op jit(solution)/shard_map/ppermute | solution.py:136
  66.8 4.7 %collective-permute-start.14 = (bf16[1,1,1,8,512]{4,3,0,2,1:T(8,128)(2,1)S(1)}, bf16[1,1,1,8,512]{4,3,0,2,1:T(8,128)(2,1)S(1)}, u32[]{:S(2)}, u32[]{:S(2)}) collective-permute-start(bf16[1,1,1,8,512]{4,3,0,2,1:T(8,128)(2,1)S(1)} %get-tuple-element.104), channel_id=1, source_target_pairs={{0,15},{1,0},{2,1},{3,2},{4,3},{5,4},{6,5},{7,6},{8,7},{9,8},{10,9... | collective-permute-start | bytes 24584 | tf_op jit(solution)/shard_map/ppermute | solution.py:136
